TPU v7x, 32 devices: a whole 2x2x4 slice. The times are simulated.
32 devices in a mesh: img: 4 (over x, core), cls: 4 (over z), tpl: 2 (over y).
Axes of the slice: x: 2, y: 2, z: 4, core: 2. Of those that a mesh axis runs over, the one named last changes fastest.
Arguments:
- images: bfloat16 [2048, 1280], P(('img', 'tpl')), may hold values from -5 to 5
- labels: int32 [2048], P(('img', 'tpl')), may hold values from 0 to 1023
- templates: bfloat16 [8, 1024, 1280], P('tpl', ('cls', 'img')), may hold values from -0.125 to 0.125
- projection: bfloat16 [1280, 1280], P('img', 'cls'), may hold values from -0.08441157 to 0.08441157
Outputs:
- grad_templates: bfloat16 [8, 1024, 1280], P('tpl', ('cls', 'img'))
- grad_projection: float32 [1280, 1280], P('img', 'cls')
All inputs are finite; a program needn't handle non-finite values.
Results may differ from a plain program's by a relative error of at most 0.011.
Values may be sent and summed in bfloat16 or wider, within the bound.
No kernel may reach another device: no remote copies, remote signals or barrier semaphores. Data moves between devices by JAX's collectives and lax.ppermute only.
A program may use at most 64 MiB of HBM per device.

v0:
```python
import jax
import jax.numpy as jnp
from jax import lax
from jax.sharding import PartitionSpec as P

logit_scale = 50.0
epsilon = 1e-06


def inverse_norm(values):
    return lax.rsqrt(jnp.sum(values * values, axis=-1, keepdims=True) + epsilon)


def body(images, labels, templates, projection):
    tpl_count = templates.shape[0]
    cls_count = templates.shape[1]
    feat_width = templates.shape[2]
    tpl_total = tpl_count * lax.axis_size("tpl")
    img_count = lax.axis_size("img")
    wide_proj = lax.all_gather(projection, "cls", axis=1, tiled=True)
    full_proj = lax.all_gather(wide_proj, "img", axis=0, tiled=True)
    flat_tpl = templates.reshape(tpl_count * cls_count, feat_width)
    text_z = jnp.dot(flat_tpl, full_proj, preferred_element_type=jnp.float32)
    text_rz = inverse_norm(text_z)
    text_u = text_z * text_rz
    u_three = text_u.reshape(tpl_count, cls_count, feat_width)
    local_sum = jnp.sum(u_three, axis=0)
    mean_emb = lax.psum(local_sum, "tpl") / tpl_total
    mean_rn = inverse_norm(mean_emb)
    class_w = mean_emb * mean_rn
    class_b = class_w.astype(jnp.bfloat16)
    img_f = images.astype(jnp.float32)
    img_b = (img_f * inverse_norm(img_f)).astype(jnp.bfloat16)
    class_panel = lax.all_gather(class_b, "img", axis=0, tiled=True)
    scores = logit_scale * jnp.einsum(
        "cd,nd->cn", class_panel, img_b, preferred_element_type=jnp.float32
    )
    exp_scores = jnp.exp(scores)
    totals = lax.psum(jnp.sum(exp_scores, axis=0), "cls")
    first_id = lax.axis_index("cls") * img_count * cls_count
    class_ids = first_id + lax.broadcasted_iota(jnp.int32, (class_panel.shape[0], 1), 0)
    one_hot = (labels[None, :] == class_ids).astype(jnp.float32)
    grad_logit = (exp_scores / totals[None, :] - one_hot).astype(jnp.bfloat16)
    spread = lax.psum_scatter(
        logit_scale * jnp.dot(grad_logit, img_b, preferred_element_type=jnp.float32),
        "img",
        scatter_dimension=0,
        tiled=True,
    )
    class_g = lax.psum(spread, "tpl")
    dot_wg = jnp.sum(class_w * class_g, axis=1, keepdims=True)
    grad_mean = (class_g - class_w * dot_wg) * mean_rn
    per_u = grad_mean / tpl_total
    inner_prod = jnp.sum(u_three * per_u[None], axis=2, keepdims=True)
    grad_z = (
        (per_u[None] - u_three * inner_prod) * text_rz.reshape(tpl_count, cls_count, 1)
    ).astype(jnp.bfloat16)
    grad_flat = grad_z.reshape(tpl_count * cls_count, feat_width)
    grad_tpl = lax.dot_general(
        grad_flat, full_proj, (((1,), (1,)), ((), ())), preferred_element_type=jnp.float32
    )
    grad_templates = grad_tpl.astype(jnp.bfloat16).reshape(tpl_count, cls_count, feat_width)
    tpl_columns = lax.all_to_all(flat_tpl, "img", split_axis=1, concat_axis=0, tiled=True)
    partial_proj = lax.dot_general(
        tpl_columns,
        lax.all_gather(grad_flat, "img", axis=0, tiled=True),
        (((0,), (0,)), ((), ())),
        preferred_element_type=jnp.float32,
    )
    shared_proj = lax.psum_scatter(
        partial_proj.astype(jnp.bfloat16), "cls", scatter_dimension=1, tiled=True
    )
    grad_projection = lax.psum(shared_proj, "tpl").astype(jnp.float32)
    return (grad_templates, grad_projection)


def solution(mesh):
    in_specs = (
        P(("img", "tpl"), None),
        P(("img", "tpl")),
        P("tpl", ("cls", "img"), None),
        P("img", "cls"),
    )
    out_specs = (P("tpl", ("cls", "img"), None), P("img", "cls"))
    return jax.shard_map(body, mesh=mesh, in_specs=in_specs, out_specs=out_specs, check_vma=False)
```

profile of v0, /device:TPU:0, one launch (start us, length us, event | category | flops | bytes accessed | tf_op | source)
XLA Modules:
  0.0 261.0 jit_solution(5731900698816479913)
XLA Ops:
  7.2 0.0 all-gather.3.cloned.1.call-start
  7.2 1.1 copy.10
  8.3 23.5 %all_gather.12 = bf16[320,1280]{0,1:T(8,128)(2,1)S(1)} all-gather(bf16[320,320]{0,1:T(8,128)(2,1)S(1)} %copy.10), channel_id=1, replica_groups=mesh['img'=4,'cls'=4,'tpl'=2] {'cls'}, dimensions={1}, use_global_device_ids=true | all-gather | bytes 1024000 | tf_op jit(solution)/shard_map/all_gather | solution.py:20
  31.8 1.3 copy.11
  33.1 0.0 all-gather.3.cloned.1.call-update
  33.1 0.0 all-reduce.4.cloned.1.call-start
  33.2 0.2 fusion.1
  33.4 29.0 %all-gather.3.cloned.1.call-done = bf16[1280,1280]{1,0:T(8,128)(2,1)} async-done(((bf16[320,1280]{1,0:T(8,128)(2,1)}), bf16[1280,1280]{1,0:T(8,128)(2,1)}) %all-gather.3.cloned.1.call-update) | async-done | bytes 3276816 | tf_op jit(solution)/shard_map/all_gather | solution.py:21
  62.4 3.0 %multiply_reduce_fusion = (f32[256]{0:T(256)S(1)}, f32[256,1280]{1,0:T(8,128)S(1)}) fusion(bf16[256,1280]{1,0:T(8,128)(2,1)S(1)} %bitcast.29, bf16[1280,1280]{1,0:T(8,128)(2,1)} %all-gather.3.cloned.1.call-done), kind=kOutput, calls=%fused_computation.13 | convolution fusion | flops 839515904 | bytes 5243904 | tf_op jit(solution)/shard_map/dot_general | solution.py:23
  65.5 0.2 broadcast_multiply_fusion
  65.7 0.8 reduce_sum.64
  66.5 0.0 all-reduce.4.cloned.1.call-update
  66.5 0.0 reduce-scatter.5.cloned.1.call-start
  66.6 24.4 %all-reduce.4.cloned.1.call-done = f32[64,1280]{1,0:T(8,128)} async-done(((f32[64,1280]{1,0:T(8,128)}), f32[64,1280]{1,0:T(8,128)}) %all-reduce.4.cloned.1.call-update) | async-done | bytes 327696 | tf_op jit(solution)/shard_map/psum | solution.py:28
  91.0 1.1 multiply_reduce_fusion.2
  92.1 1.1 multiply_convert_fusion
  93.2 0.0 copy-start.5
  93.2 7.9 %all_gather.14 = bf16[256,1280]{1,0:T(8,128)(2,1)S(1)} all-gather(bf16[64,1280]{1,0:T(8,128)(2,1)S(1)} %multiply_convert_fusion), channel_id=1, replica_groups=mesh['img'=4,'cls'=4,'tpl'=2] {'img'}, dimensions={0}, use_global_device_ids=true | all-gather | bytes 819200 | tf_op jit(solution)/shard_map/all_gather | solution.py:34
  101.1 0.5 fusion.12
  101.5 11.7 %psum.29 = f32[256]{0:T(256)S(1)} all-reduce(f32[256]{0:T(256)S(1)} %get-tuple-element.6), channel_id=1, replica_groups=mesh['img'=4,'cls'=4,'tpl'=2] {'cls'}, use_global_device_ids=true, to_apply=%region_6.0 | all-reduce | flops 256 | bytes 2048 | tf_op jit(solution)/shard_map/psum | solution.py:39
  113.2 1.5 convolution_multiply_fusion
  114.7 0.0 reduce-scatter.5.cloned.1.call-update
  114.8 0.0 all-reduce.6.cloned.1.call-start
  114.8 23.3 %reduce-scatter.5.cloned.1.call-done = f32[64,1280]{1,0:T(8,128)} async-done(((f32[256,1280]{1,0:T(8,128)}), f32[64,1280]{1,0:T(8,128)}) %reduce-scatter.5.cloned.1.call-update) | async-done | bytes 327696 | tf_op jit(solution)/shard_map/reduce_scatter | solution.py:44
  138.1 0.0 all-reduce.6.cloned.1.call-update
  138.1 0.0 all-gather.5.cloned.1.call-start
  138.2 26.4 %all-reduce.6.cloned.1.call-done = f32[64,1280]{1,0:T(8,128)} async-done(((f32[64,1280]{1,0:T(8,128)}), f32[64,1280]{1,0:T(8,128)}) %all-reduce.6.cloned.1.call-update) | async-done | bytes 327696 | tf_op jit(solution)/shard_map/psum | solution.py:50
  164.6 1.2 multiply_reduce_fusion.1
  165.8 1.1 multiply_multiply_fusion
  166.9 0.3 fusion.3
  167.2 1.1 fusion.5
  168.4 0.0 all-gather.5.cloned.1.call-update
  168.4 0.0 reduce-scatter.7.cloned.1.call-start
  168.4 0.9 all_to_all.14
  169.3 0.6 copy.12
  169.9 17.5 %all_to_all.19 = bf16[256,4,320]{0,2,1:T(8,128)(2,1)S(1)} all-to-all(bf16[256,4,320]{0,2,1:T(8,128)(2,1)S(1)} %copy.12), channel_id=1, replica_groups=mesh['img'=4,'cls'=4,'tpl'=2] {'img'}, dimensions={1} | all-to-all | bytes 1310720 | tf_op jit(solution)/shard_map/all_to_all | solution.py:63
  187.4 0.1 copy.16
  187.5 10.8 %all-gather.5.cloned.1.call-done = bf16[1024,1280]{1,0:T(8,128)(2,1)} async-done(((bf16[256,1280]{1,0:T(8,128)(2,1)}), bf16[1024,1280]{1,0:T(8,128)(2,1)}) %all-gather.5.cloned.1.call-update) | async-done | bytes 2621456 | tf_op jit(solution)/shard_map/all_gather | solution.py:66
  198.3 2.7 %fusion = bf16[320,1280]{1,0:T(8,128)(2,1)S(1)} fusion(bf16[1024,320]{0,1:T(8,128)(2,1)S(1)} %bitcast.30, bf16[1024,1280]{1,0:T(8,128)(2,1)} %all-gather.5.cloned.1.call-done), kind=kOutput, calls=%fused_computation.3 | convolution fusion | flops 839270400 | bytes 4096000 | tf_op jit(solution)/shard_map/dot_general | solution.py:64
  201.0 1.3 copy.14
  202.4 0.0 reduce-scatter.7.cloned.1.call-update
  202.4 0.0 all-reduce.8.cloned.1.call-start
  202.4 25.5 %reduce-scatter.7.cloned.1.call-done = bf16[320,320]{1,0:T(8,128)(2,1)} async-done(((bf16[1280,320]{1,0:T(8,128)(2,1)}), bf16[320,320]{1,0:T(8,128)(2,1)}) %reduce-scatter.7.cloned.1.call-update) | async-done | bytes 204816
  227.9 1.8 copy.15
  229.7 0.0 all-reduce.8.cloned.1.call-update
  229.7 3.8 %convolution_convert_fusion.1 = bf16[256,1280]{1,0:T(8,128)(2,1)} fusion(bf16[256,1280]{1,0:T(8,128)(2,1)S(1)} %copy-done.1, bf16[1280,1280]{1,0:T(8,128)(2,1)} %all-gather.3.cloned.1.call-done), kind=kOutput, calls=%fused_computation.2 | convolution fusion | flops 839188480 | bytes 4587520 | tf_op jit(solution)/shard_map/dot_general | solution.py:59
  233.5 18.9 %all-reduce.8.cloned.1.call-done = bf16[320,320]{1,0:T(8,128)(2,1)} async-done(((bf16[320,320]{1,0:T(8,128)(2,1)}), bf16[320,320]{1,0:T(8,128)(2,1)}) %all-reduce.8.cloned.1.call-update) | async-done | bytes 204816 | tf_op jit(solution)/shard_map/psum | solution.py:73
  252.4 1.8 convert_element_type.40
  (15 shorter events, 0.0 us)
Async XLA Ops:
  7.2 55.3 %all-gather.3.cloned.1.call-start = ((), (), s32[]{:S(2)}) async-start(), calls=%async_computation.3 | async-start | bytes 4096000 | tf_op jit(solution)/shard_map/all_gather | solution.py:21
  31.8 1.4 copy-start.2
  31.8 30.6 %copy-start.3 = (bf16[4,64,1280]{2,1,0:T(8,128)(2,1)S(1)}, bf16[4,64,1280]{2,1,0:T(8,128)(2,1)}, u32[]{:S(2)}) copy-start(bf16[4,64,1280]{2,1,0:T(8,128)(2,1)} %param.6) | copy-start | bytes 1966084
  33.1 57.9 %all-reduce.4.cloned.1.call-start = ((), (), s32[]{:S(2)}) async-start(), calls=%async_computation.4 | async-start | bytes 655360 | tf_op jit(solution)/shard_map/psum | solution.py:28
  66.5 71.6 %reduce-scatter.5.cloned.1.call-start = ((), (), s32[]{:S(2)}) async-start(), calls=%async_computation.5 | async-start | bytes 1638400 | tf_op jit(solution)/shard_map/reduce_scatter | solution.py:44
  93.2 20.1 %copy-start.5 = (s32[256]{0:T(256)S(1)}, s32[256]{0:T(256)}, u32[]{:S(2)}) copy-start(s32[256]{0:T(256)} %param.5) | copy-start | bytes 3076
  114.7 49.9 %copy-start = (f32[64,1280]{1,0:T(8,128)S(1)}, f32[64,1280]{1,0:T(8,128)}, u32[]{:S(2)}) copy-start(f32[64,1280]{1,0:T(8,128)} %all-reduce.4.cloned.1.call-done) | copy-start | bytes 983044
  114.8 49.8 %all-reduce.6.cloned.1.call-start = ((), (), s32[]{:S(2)}) async-start(), calls=%async_computation.6 | async-start | bytes 655360 | tf_op jit(solution)/shard_map/psum | solution.py:50
  138.1 60.2 %all-gather.5.cloned.1.call-start = ((), (), s32[]{:S(2)}) async-start(), calls=%async_computation.7 | async-start | bytes 3276800 | tf_op jit(solution)/shard_map/all_gather | solution.py:66
  167.2 1.2 copy-start.4
  168.4 59.5 %reduce-scatter.7.cloned.1.call-start = ((), (), s32[]{:S(2)}) async-start(), calls=%async_computation.9 | async-start | bytes 1228800
  202.3 27.4 %copy-start.1 = (bf16[256,1280]{1,0:T(8,128)(2,1)S(1)}, bf16[256,1280]{1,0:T(8,128)(2,1)}, u32[]{:S(2)}) copy-start(bf16[256,1280]{1,0:T(8,128)(2,1)} %fusion.5) | copy-start | bytes 1966084
  202.4 50.0 %all-reduce.8.cloned.1.call-start = ((), (), s32[]{:S(2)}) async-start(), calls=%async_computation.8 | async-start | bytes 491520 | tf_op jit(solution)/shard_map/psum | solution.py:73
Sparse Core Ops, SparseCore 0:
  33.2 29.1 all-gather.2
  66.6 24.3 all-reduce.3
  114.9 23.1 reduce-scatter.4
  140.2 24.3 all-reduce.5
  168.5 29.7 all-gather.4
  202.5 25.3 reduce-scatter.6
  230.7 21.6 all-reduce.7
where the time goes:
time: 262 us; the launch traced here: 261 us
  waiting for transfers between devices  158 us (60%)
  blocking collectives  60.5 us (23%)
  between operations  14.3 us (5%)
  matrix products  11.6 us (4%)
  other arithmetic  8.86 us (3%)
  local copies, waits for them, and re-layouts  7.09 us (3%)
    all_gather x1, waiting for transfers between devices, body(): full_proj = lax.all_gather(wide_proj, 'img', axis=0, tiled=True)  29 us
    psum x1, waiting for transfers between devices, body(): class_g = lax.psum(spread, 'tpl')  26.4 us
    unnamed x8, waiting for transfers between devices  25.6 us
    psum x1, waiting for transfers between devices, body(): mean_emb = lax.psum(local_sum, 'tpl') / tpl_total  24.4 us
    all_gather x1, blocking collectives, body(): wide_proj = lax.all_gather(projection, 'cls', axis=1, tiled=True)  23.5 us
    reduce_scatter x1, waiting for transfers between devices, body(): lax.psum_scatter(logit_scale * jnp.dot(grad_logit, img_b, preferred_eleme...  23.3 us
    psum x1, waiting for transfers between devices, body(): grad_projection = lax.psum(shared_proj, 'tpl').astype(jnp.float32)  18.9 us
    all_to_all x1, blocking collectives, body(): lax.all_to_all(flat_tpl, 'img', split_axis=1, concat_axis=0, tiled=True)  17.5 us
  transfers between devices with their start and end apart: 7, of which 7 were waited for; matrix products, arithmetic and copies ran while one was open for 2% of the time, Pallas kernels for 0%

commit v1 on v0

--- a/solution.py
+++ b/solution.py
@@ -25,7 +25,7 @@
     text_u = text_z * text_rz
     u_three = text_u.reshape(tpl_count, cls_count, feat_width)
     local_sum = jnp.sum(u_three, axis=0)
-    mean_emb = lax.psum(local_sum, "tpl") / tpl_total
+    mean_emb = jnp.sum(lax.all_gather(local_sum, "tpl"), axis=0) / tpl_total
     mean_rn = inverse_norm(mean_emb)
     class_w = mean_emb * mean_rn
     class_b = class_w.astype(jnp.bfloat16)

time: 262 us -> 245 us (0.935)
  waiting for transfers between devices: 158 us -> 135 us
  blocking collectives: 60.5 us -> 70.2 us
  other arithmetic: 8.86 us -> 6.23 us
    psum x1 -> x0, waiting for transfers between devices: 24.4 us -> none  [body(): mean_emb = lax.psum(local_sum, 'tpl') / tpl_total]
    all_gather x0 -> x1, blocking collectives: none -> 10.5 us  [body(): mean_emb = jnp.sum(lax.all_gather(local_sum, 'tpl'), axis=0) / tpl_total]
    unnamed x8 -> x7, waiting for transfers between devices: 25.6 us -> 25.6 us
  transfers between devices with their start and end apart: 7 -> 6, of which waited for: 7 -> 6; matrix products, arithmetic and copies ran while one was open for 2% -> 2% of each run, Pallas kernels for 0% -> 0%
where the time goes in v1:
time: 245 us
  waiting for transfers between devices  135 us (55%)
  blocking collectives  70.2 us (29%)
  between operations  14.2 us (6%)
  matrix products  11.6 us (5%)
  local copies, waits for them, and re-layouts  7.09 us (3%)
  other arithmetic  6.23 us (3%)
    all_gather x1, waiting for transfers between devices, body(): full_proj = lax.all_gather(wide_proj, 'img', axis=0, tiled=True)  29 us
    psum x1, waiting for transfers between devices, body(): class_g = lax.psum(spread, 'tpl')  26.6 us
    unnamed x7, waiting for transfers between devices  25.6 us
    reduce_scatter x1, waiting for transfers between devices, body(): lax.psum_scatter(logit_scale * jnp.dot(grad_logit, img_b, preferred_eleme...  24.6 us
    all_gather x1, blocking collectives, body(): wide_proj = lax.all_gather(projection, 'cls', axis=1, tiled=True)  23.5 us
    psum x1, waiting for transfers between devices, body(): grad_projection = lax.psum(shared_proj, 'tpl').astype(jnp.float32)  18.7 us
    all_to_all x1, blocking collectives, body(): lax.all_to_all(flat_tpl, 'img', split_axis=1, concat_axis=0, tiled=True)  17.5 us
    psum x1, blocking collectives, body(): totals = lax.psum(jnp.sum(exp_scores, axis=0), 'cls')  11.7 us
  transfers between devices with their start and end apart: 6, of which 6 were waited for; matrix products, arithmetic and copies ran while one was open for 2% of the time, Pallas kernels for 0%

profile of v1, /device:TPU:0, one launch (start us, length us, event | category | flops | bytes accessed | tf_op | source)
XLA Modules:
  0.0 244.8 jit_solution(15652575733572654541)
XLA Ops:
  7.2 0.0 all-gather.4.cloned.1.call-start
  7.2 1.1 copy.14
  8.3 23.5 %all_gather.18 = bf16[320,1280]{0,1:T(8,128)(2,1)S(1)} all-gather(bf16[320,320]{0,1:T(8,128)(2,1)S(1)} %copy.14), channel_id=1, replica_groups=mesh['img'=4,'cls'=4,'tpl'=2] {'cls'}, dimensions={1}, use_global_device_ids=true | all-gather | bytes 1024000 | tf_op jit(solution)/shard_map/all_gather | solution.py:20
  31.8 1.3 copy.15
  33.1 0.0 all-gather.4.cloned.1.call-update
  33.1 0.0 reduce-scatter.5.cloned.1.call-start
  33.2 0.0 copy-done.1
  33.2 0.2 fusion.1
  33.4 29.0 %all-gather.4.cloned.1.call-done = bf16[1280,1280]{1,0:T(8,128)(2,1)} async-done(((bf16[320,1280]{1,0:T(8,128)(2,1)}), bf16[1280,1280]{1,0:T(8,128)(2,1)}) %all-gather.4.cloned.1.call-update) | async-done | bytes 3276816 | tf_op jit(solution)/shard_map/all_gather | solution.py:21
  62.4 3.0 %multiply_reduce_fusion = (f32[256]{0:T(256)S(1)}, f32[256,1280]{1,0:T(8,128)S(1)}) fusion(bf16[256,1280]{1,0:T(8,128)(2,1)S(1)} %bitcast.31, bf16[1280,1280]{1,0:T(8,128)(2,1)} %all-gather.4.cloned.1.call-done), kind=kOutput, calls=%fused_computation.13 | convolution fusion | flops 839515904 | bytes 5243904 | tf_op jit(solution)/shard_map/dot_general | solution.py:23
  65.5 0.2 broadcast_multiply_fusion
  65.7 0.1 reduce_sum.73
  65.8 10.5 %all-gather = f32[128,1280]{1,0:T(8,128)S(1)} all-gather(f32[64,1280]{1,0:T(8,128)S(1)} %reduce_sum.73), channel_id=2, replica_groups=mesh['img'=4,'cls'=4,'tpl'=2] {'tpl'}, dimensions={0}, use_global_device_ids=true | all-gather | bytes 983040 | tf_op jit(solution)/shard_map/all_gather | solution.py:28
  76.3 0.1 multiply_reduce_fusion.2
  76.5 0.1 multiply_convert_fusion
  76.6 0.0 copy-start.5
  76.6 7.0 %all_gather.22 = bf16[256,1280]{1,0:T(8,128)(2,1)S(1)} all-gather(bf16[64,1280]{1,0:T(8,128)(2,1)S(1)} %multiply_convert_fusion), channel_id=1, replica_groups=mesh['img'=4,'cls'=4,'tpl'=2] {'img'}, dimensions={0}, use_global_device_ids=true | all-gather | bytes 819200 | tf_op jit(solution)/shard_map/all_gather | solution.py:34
  83.6 0.5 fusion.12
  84.1 11.7 %psum.21 = f32[256]{0:T(256)S(1)} all-reduce(f32[256]{0:T(256)S(1)} %get-tuple-element.6), channel_id=1, replica_groups=mesh['img'=4,'cls'=4,'tpl'=2] {'cls'}, use_global_device_ids=true, to_apply=%region_6.0 | all-reduce | flops 256 | bytes 2048 | tf_op jit(solution)/shard_map/psum | solution.py:39
  95.8 1.5 convolution_multiply_fusion
  97.3 0.0 reduce-scatter.5.cloned.1.call-update
  97.3 0.0 all-reduce.3.cloned.1.call-start
  97.3 24.6 %reduce-scatter.5.cloned.1.call-done = f32[64,1280]{1,0:T(8,128)} async-done(((f32[256,1280]{1,0:T(8,128)}), f32[64,1280]{1,0:T(8,128)}) %reduce-scatter.5.cloned.1.call-update) | async-done | bytes 327696 | tf_op jit(solution)/shard_map/reduce_scatter | solution.py:44
  121.9 0.0 all-reduce.3.cloned.1.call-update
  121.9 0.0 all-gather.6.cloned.1.call-start
  122.0 26.6 %all-reduce.3.cloned.1.call-done = f32[64,1280]{1,0:T(8,128)} async-done(((f32[64,1280]{1,0:T(8,128)}), f32[64,1280]{1,0:T(8,128)}) %all-reduce.3.cloned.1.call-update) | async-done | bytes 327696 | tf_op jit(solution)/shard_map/psum | solution.py:50
  148.6 1.2 multiply_reduce_fusion.1
  149.8 1.1 multiply_multiply_fusion
  150.9 0.3 fusion.3
  151.2 0.0 copy-start.4
  151.2 1.1 fusion.5
  152.3 0.0 all-gather.6.cloned.1.call-update
  152.3 0.0 reduce-scatter.7.cloned.1.call-start
  152.4 0.9 all_to_all.14
  153.3 0.6 copy.16
  153.9 17.5 %all_to_all.19 = bf16[256,4,320]{0,2,1:T(8,128)(2,1)S(1)} all-to-all(bf16[256,4,320]{0,2,1:T(8,128)(2,1)S(1)} %copy.16), channel_id=1, replica_groups=mesh['img'=4,'cls'=4,'tpl'=2] {'img'}, dimensions={1} | all-to-all | bytes 1310720 | tf_op jit(solution)/shard_map/all_to_all | solution.py:63
  171.4 0.1 copy.20
  171.5 10.8 %all-gather.6.cloned.1.call-done = bf16[1024,1280]{1,0:T(8,128)(2,1)} async-done(((bf16[256,1280]{1,0:T(8,128)(2,1)}), bf16[1024,1280]{1,0:T(8,128)(2,1)}) %all-gather.6.cloned.1.call-update) | async-done | bytes 2621456 | tf_op jit(solution)/shard_map/all_gather | solution.py:66
  182.3 2.7 %fusion = bf16[320,1280]{1,0:T(8,128)(2,1)S(1)} fusion(bf16[1024,320]{0,1:T(8,128)(2,1)S(1)} %bitcast.32, bf16[1024,1280]{1,0:T(8,128)(2,1)} %all-gather.6.cloned.1.call-done), kind=kOutput, calls=%fused_computation.3 | convolution fusion | flops 839270400 | bytes 4096000 | tf_op jit(solution)/shard_map/dot_general | solution.py:64
  185.0 1.3 copy.18
  186.3 0.0 reduce-scatter.7.cloned.1.call-update
  186.3 0.0 all-reduce.5.cloned.1.call-start
  186.4 25.5 %reduce-scatter.7.cloned.1.call-done = bf16[320,320]{1,0:T(8,128)(2,1)} async-done(((bf16[1280,320]{1,0:T(8,128)(2,1)}), bf16[320,320]{1,0:T(8,128)(2,1)}) %reduce-scatter.7.cloned.1.call-update) | async-done | bytes 204816
  211.9 1.8 copy.19
  213.7 0.0 all-reduce.5.cloned.1.call-update
  213.7 3.8 %convolution_convert_fusion.1 = bf16[256,1280]{1,0:T(8,128)(2,1)} fusion(bf16[256,1280]{1,0:T(8,128)(2,1)S(1)} %copy-done, bf16[1280,1280]{1,0:T(8,128)(2,1)} %all-gather.4.cloned.1.call-done), kind=kOutput, calls=%fused_computation.2 | convolution fusion | flops 839188480 | bytes 4587520 | tf_op jit(solution)/shard_map/dot_general | solution.py:59
  217.5 18.7 %all-reduce.5.cloned.1.call-done = bf16[320,320]{1,0:T(8,128)(2,1)} async-done(((bf16[320,320]{1,0:T(8,128)(2,1)}), bf16[320,320]{1,0:T(8,128)(2,1)}) %all-reduce.5.cloned.1.call-update) | async-done | bytes 204816 | tf_op jit(solution)/shard_map/psum | solution.py:73
  236.2 1.8 convert_element_type.40
  (14 shorter events, 0.1 us)
Async XLA Ops:
  7.2 55.3 %all-gather.4.cloned.1.call-start = ((), (), s32[]{:S(2)}) async-start(), calls=%async_computation.3 | async-start | bytes 4096000 | tf_op jit(solution)/shard_map/all_gather | solution.py:21
  31.8 1.4 copy-start.1
  31.8 30.6 %copy-start.3 = (bf16[4,64,1280]{2,1,0:T(8,128)(2,1)S(1)}, bf16[4,64,1280]{2,1,0:T(8,128)(2,1)}, u32[]{:S(2)}) copy-start(bf16[4,64,1280]{2,1,0:T(8,128)(2,1)} %param.6) | copy-start | bytes 1966084
  33.1 88.8 %reduce-scatter.5.cloned.1.call-start = ((), (), s32[]{:S(2)}) async-start(), calls=%async_computation.4 | async-start | bytes 1638400 | tf_op jit(solution)/shard_map/reduce_scatter | solution.py:44
  76.3 7.3 %copy-start.2 = (bf16[256,1280]{1,0:T(8,128)(2,1)S(1)}, bf16[256,1280]{1,0:T(8,128)(2,1)}, u32[]{:S(2)}) copy-start(bf16[256,1280]{1,0:T(8,128)(2,1)} %param.4) | copy-start | bytes 1966084
  76.6 19.2 %copy-start.5 = (s32[256]{0:T(256)S(1)}, s32[256]{0:T(256)}, u32[]{:S(2)}) copy-start(s32[256]{0:T(256)} %param.5) | copy-start | bytes 3076
  97.3 51.3 %all-reduce.3.cloned.1.call-start = ((), (), s32[]{:S(2)}) async-start(), calls=%async_computation.5 | async-start | bytes 655360 | tf_op jit(solution)/shard_map/psum | solution.py:50
  121.9 60.3 %all-gather.6.cloned.1.call-start = ((), (), s32[]{:S(2)}) async-start(), calls=%async_computation.6 | async-start | bytes 3276800 | tf_op jit(solution)/shard_map/all_gather | solution.py:66
  151.2 1.2 copy-start.4
  152.3 59.5 %reduce-scatter.7.cloned.1.call-start = ((), (), s32[]{:S(2)}) async-start(), calls=%async_computation.8 | async-start | bytes 1228800
  186.3 27.4 %copy-start = (bf16[256,1280]{1,0:T(8,128)(2,1)S(1)}, bf16[256,1280]{1,0:T(8,128)(2,1)}, u32[]{:S(2)}) copy-start(bf16[256,1280]{1,0:T(8,128)(2,1)} %fusion.5) | copy-start | bytes 1966084
  186.3 49.9 %all-reduce.5.cloned.1.call-start = ((), (), s32[]{:S(2)}) async-start(), calls=%async_computation.7 | async-start | bytes 491520 | tf_op jit(solution)/shard_map/psum | solution.py:73
Sparse Core Ops, SparseCore 0:
  33.2 29.1 all-gather.3
  97.4 24.4 reduce-scatter.4
  124.2 24.3 all-reduce.2
  152.5 29.7 all-gather.5
  186.5 25.3 reduce-scatter.6
  214.6 21.6 all-reduce.4
